TPU v7x, 32 devices: a whole 2x2x4 slice. The times are simulated.
32 devices in a mesh: shard: 16 (over z, x, core), replica: 2 (over y).
Axes of the slice: x: 2, y: 2, z: 4, core: 2. Of those that a mesh axis runs over, the one named last changes fastest.
Arguments:
- x_in: bfloat16 [2, 8192, 768], P('replica', 'shard'), may hold values from -6 to 6
- seq_units: int32 [2, 16], P('replica'), may hold values from 1 to 64, 512 in all within a row
- deal: int32 [2, 16], P('replica'), may hold values from 0 to 15, each once within a row
- gain_attn: float32 [768], replicated, may hold values from 0.1 to 1.9
- w_query: bfloat16 [768, 768], P('shard'), may hold values from -0.4375 to 0.4375
- w_key: bfloat16 [768, 768], P('shard'), may hold values from -0.21875 to 0.21875
- w_value: bfloat16 [768, 768], P('shard'), may hold values from -0.21875 to 0.21875
- w_out: bfloat16 [768, 768], P('shard'), may hold values from -0.875 to 0.875
- gain_ffn: float32 [768], replicated, may hold values from 0.1 to 1.9
- w_gate: bfloat16 [768, 2048], P('shard'), may hold values from -0.21875 to 0.21875
- w_up: bfloat16 [768, 2048], P('shard'), may hold values from -0.21875 to 0.21875
- w_down: bfloat16 [2048, 768], P('shard'), may hold values from -0.125 to 0.125
- d_out: bfloat16 [2, 16, 1024, 768], P('replica', 'shard'), may hold values from -6 to 6
Outputs:
- layer_out: bfloat16 [2, 16, 1024, 768], P('replica', 'shard')
- grad_x: bfloat16 [2, 8192, 768], P('replica', 'shard')
- grad_gain_attn: float32 [768], P('shard')
- grad_gain_ffn: float32 [768], P('shard')
- grad_w_query: float32 [768, 768], P('shard')
- grad_w_key: float32 [768, 768], P('shard')
- grad_w_value: float32 [768, 768], P('shard')
- grad_w_out: float32 [768, 768], P('shard')
- grad_w_gate: float32 [768, 2048], P('shard')
- grad_w_up: float32 [768, 2048], P('shard')
- grad_w_down: float32 [2048, 768], P('shard')
Inputs may be any that keep to these rules, and one draw needn't show every extreme that they name: `seq_units`: each group's 16 entries sum to 512. `deal`: each group's row names every sequence 0 to 15 once.
All inputs are finite; a program needn't handle non-finite values.
Results may differ from a plain program's by a relative error of at most 0.023.
Values may be sent and summed in bfloat16 or wider, within the bound.
No kernel may reach another device: no remote copies, remote signals or barrier semaphores. Data moves between devices by JAX's collectives and lax.ppermute only.
A program may use at most 320 MiB of HBM per device.

v0:
```python
import jax
import jax.numpy as jnp
from jax import lax
from jax.sharding import PartitionSpec as P

H = 12
HD = 64
norm_eps = 1e-06
neg_big = -1e30


def rms_scale(tok_rows, gain_vec):
    inverse = lax.rsqrt(jnp.mean(tok_rows * tok_rows, axis=-1, keepdims=True) + norm_eps)
    return tok_rows * inverse * gain_vec


def gelu_mix(gate_vals, up_vals):
    return jax.nn.gelu(gate_vals, approximate=True) * up_vals


def lookup(table, wanted):
    table_slots = jnp.arange(table.shape[0], dtype=jnp.int32)
    return jnp.sum(jnp.where(wanted[:, None] == table_slots[None, :], table[None, :], 0), axis=1)


def left_dot(lhs_mat, rhs_mat):
    return lax.dot_general(
        lhs_mat, rhs_mat, (((0,), (0,)), ((), ())), preferred_element_type=jnp.float32
    )


def right_dot(lhs_mat, rhs_mat):
    return lax.dot_general(
        lhs_mat, rhs_mat, (((1,), (1,)), ((), ())), preferred_element_type=jnp.float32
    )


def plain_dot(lhs_mat, rhs_mat):
    return jnp.dot(lhs_mat, rhs_mat, preferred_element_type=jnp.float32)


def attend_forward(queries, keys_all, values_all, live_keys):
    total_rows = queries.shape[0]
    row_block = min(512, total_rows)
    factor = HD ** (-0.5)
    key_heads = keys_all.reshape(total_rows, H, HD)
    value_heads = values_all.reshape(total_rows, H, HD)
    mixed_list = []
    stat_list = []
    for row_begin in range(0, total_rows, row_block):
        query_heads = queries[row_begin : row_begin + row_block].reshape(row_block, H, HD)
        scores = (
            jnp.einsum("qhd,khd->hqk", query_heads, key_heads, preferred_element_type=jnp.float32)
            * factor
        )
        scores = jnp.where(live_keys[None, None, :], scores, neg_big)
        row_max = jnp.max(scores, axis=-1, keepdims=True)
        exp_vals = jnp.exp(scores - row_max)
        row_total = jnp.sum(exp_vals, axis=-1, keepdims=True)
        prob_vals = (exp_vals / row_total).astype(jnp.bfloat16)
        mixed_rows = jnp.einsum(
            "hqk,khd->qhd", prob_vals, value_heads, preferred_element_type=jnp.float32
        )
        mixed_list.append(mixed_rows.reshape(row_block, H * HD))
        stat_list.append(row_max + jnp.log(row_total))
    return (jnp.concatenate(mixed_list, axis=0), jnp.concatenate(stat_list, axis=1))


def attend_backward(queries, keys_all, values_all, live_keys, log_totals, grad_mixed):
    total_rows = queries.shape[0]
    row_block = min(512, total_rows)
    factor = HD ** (-0.5)
    key_heads = keys_all.reshape(total_rows, H, HD)
    value_heads = values_all.reshape(total_rows, H, HD)
    grad_keys = jnp.zeros((total_rows, H, HD), jnp.float32)
    grad_values = jnp.zeros((total_rows, H, HD), jnp.float32)
    query_list = []
    for row_begin in range(0, total_rows, row_block):
        query_heads = queries[row_begin : row_begin + row_block].reshape(row_block, H, HD)
        grad_heads = grad_mixed[row_begin : row_begin + row_block].reshape(row_block, H, HD)
        scores = (
            jnp.einsum("qhd,khd->hqk", query_heads, key_heads, preferred_element_type=jnp.float32)
            * factor
        )
        scores = jnp.where(live_keys[None, None, :], scores, neg_big)
        prob_vals = jnp.exp(scores - log_totals[:, row_begin : row_begin + row_block])
        grad_probs = jnp.einsum(
            "qhd,khd->hqk", grad_heads, value_heads, preferred_element_type=jnp.float32
        )
        row_dot = jnp.sum(prob_vals * grad_probs, axis=-1, keepdims=True)
        grad_scores = (prob_vals * (grad_probs - row_dot)).astype(jnp.bfloat16)
        grad_query = (
            jnp.einsum("hqk,khd->qhd", grad_scores, key_heads, preferred_element_type=jnp.float32)
            * factor
        )
        query_list.append(grad_query.reshape(row_block, H * HD))
        grad_keys = (
            grad_keys
            + jnp.einsum(
                "hqk,qhd->khd", grad_scores, query_heads, preferred_element_type=jnp.float32
            )
            * factor
        )
        grad_values = grad_values + jnp.einsum(
            "hqk,qhd->khd",
            prob_vals.astype(jnp.bfloat16),
            grad_heads,
            preferred_element_type=jnp.float32,
        )
    return (
        jnp.concatenate(query_list, axis=0),
        grad_keys.reshape(total_rows, H * HD),
        grad_values.reshape(total_rows, H * HD),
    )


def shards(
    x_in,
    seq_units,
    deal,
    gain_attn,
    w_query,
    w_key,
    w_value,
    w_out,
    gain_ffn,
    w_gate,
    w_up,
    w_down,
    d_out,
):
    shard_count = lax.axis_size("shard")
    my_index = lax.axis_index("shard")
    width = x_in.shape[2]
    span = d_out.shape[2]
    unit_max = span // shard_count
    units_row = seq_units[0]
    order_row = deal[0]
    offsets = jnp.cumsum(units_row) - units_row
    inner_idx = jnp.arange(unit_max, dtype=jnp.int32)
    dest_idx = jnp.arange(shard_count, dtype=jnp.int32)
    counts = lookup(units_row, order_row)
    starts = lookup(offsets, order_row)
    row_index = starts[:, None] + jnp.minimum(inner_idx[None, :], counts[:, None] - 1)
    sent_live = inner_idx[None, :] < counts[:, None]
    local_rows = x_in[0]
    outgoing = jnp.where(
        sent_live[:, :, None], local_rows[row_index], jnp.zeros((), local_rows.dtype)
    )
    arrived = lax.all_to_all(outgoing, "shard", split_axis=0, concat_axis=0, tiled=True)
    own_count = jnp.sum(jnp.where(dest_idx == my_index, counts, 0))
    live_rows = jnp.broadcast_to(inner_idx[None, :] < own_count, (shard_count, unit_max)).reshape(
        span
    )
    wq_full, wk_full, wv_full, wo_full = (
        lax.all_gather(w_query, "shard", axis=0, tiled=True),
        lax.all_gather(w_key, "shard", axis=0, tiled=True),
        lax.all_gather(w_value, "shard", axis=0, tiled=True),
        lax.all_gather(w_out, "shard", axis=0, tiled=True),
    )
    tok_float = arrived.reshape(span, width).astype(jnp.float32)
    normed_one_f, norm_one_back = jax.vjp(rms_scale, tok_float, gain_attn)
    normed_one = normed_one_f.astype(jnp.bfloat16)
    queries = plain_dot(normed_one, wq_full).astype(jnp.bfloat16)
    keys_all = plain_dot(normed_one, wk_full).astype(jnp.bfloat16)
    values_all = plain_dot(normed_one, wv_full).astype(jnp.bfloat16)
    mixed_f, log_totals = attend_forward(queries, keys_all, values_all, live_rows)
    mixed_rows = mixed_f.astype(jnp.bfloat16)
    hidden_res = tok_float + plain_dot(mixed_rows, wo_full)
    wg_full, wu_full, wd_full = (
        lax.all_gather(w_gate, "shard", axis=0, tiled=True),
        lax.all_gather(w_up, "shard", axis=0, tiled=True),
        lax.all_gather(w_down, "shard", axis=0, tiled=True),
    )
    normed_two_f, norm_two_back = jax.vjp(rms_scale, hidden_res, gain_ffn)
    normed_two = normed_two_f.astype(jnp.bfloat16)
    gate_vals = plain_dot(normed_two, wg_full)
    up_vals = plain_dot(normed_two, wu_full)
    act_f, mix_back = jax.vjp(gelu_mix, gate_vals, up_vals)
    act_vals = act_f.astype(jnp.bfloat16)
    result = jnp.where(live_rows[:, None], hidden_res + plain_dot(act_vals, wd_full), 0.0)
    layer_out = result.astype(jnp.bfloat16).reshape(1, 1, span, width)
    wg_back, wu_back, wd_back = (
        lax.all_gather(w_gate, "shard", axis=0, tiled=True),
        lax.all_gather(w_up, "shard", axis=0, tiled=True),
        lax.all_gather(w_down, "shard", axis=0, tiled=True),
    )
    grad_y = jnp.where(live_rows[:, None], d_out[0, 0].astype(jnp.float32), 0.0)
    grad_ffn_b = grad_y.astype(jnp.bfloat16)
    grad_down = left_dot(act_vals, grad_ffn_b)
    grad_act = right_dot(grad_ffn_b, wd_back)
    grad_gate_f, grad_up_f = mix_back(grad_act)
    grad_gate_b = grad_gate_f.astype(jnp.bfloat16)
    grad_up_b = grad_up_f.astype(jnp.bfloat16)
    grad_wg = left_dot(normed_two, grad_gate_b)
    grad_wu = left_dot(normed_two, grad_up_b)
    grad_n2 = right_dot(grad_gate_b, wg_back) + right_dot(grad_up_b, wu_back)
    grad_h_norm, grad_gain_two = norm_two_back(grad_n2)
    ffn_share = (
        lax.psum_scatter(
            grad_wg.astype(jnp.bfloat16), "shard", scatter_dimension=0, tiled=True
        ).astype(jnp.float32),
        lax.psum_scatter(
            grad_wu.astype(jnp.bfloat16), "shard", scatter_dimension=0, tiled=True
        ).astype(jnp.float32),
        lax.psum_scatter(
            grad_down.astype(jnp.bfloat16), "shard", scatter_dimension=0, tiled=True
        ).astype(jnp.float32),
        lax.psum_scatter(
            grad_gain_two.astype(jnp.bfloat16), "shard", scatter_dimension=0, tiled=True
        ).astype(jnp.float32),
    )
    grad_hidden = grad_y + grad_h_norm
    wq_back, wk_back, wv_back, wo_back = (
        lax.all_gather(w_query, "shard", axis=0, tiled=True),
        lax.all_gather(w_key, "shard", axis=0, tiled=True),
        lax.all_gather(w_value, "shard", axis=0, tiled=True),
        lax.all_gather(w_out, "shard", axis=0, tiled=True),
    )
    grad_attn_b = grad_hidden.astype(jnp.bfloat16)
    grad_wo = left_dot(mixed_rows, grad_attn_b)
    grad_mixed = right_dot(grad_attn_b, wo_back).astype(jnp.bfloat16)
    grad_q_f, grad_k_f, grad_v_f = attend_backward(
        queries, keys_all, values_all, live_rows, log_totals, grad_mixed
    )
    grad_q_b = grad_q_f.astype(jnp.bfloat16)
    grad_k_b = grad_k_f.astype(jnp.bfloat16)
    grad_v_b = grad_v_f.astype(jnp.bfloat16)
    grad_wq = left_dot(normed_one, grad_q_b)
    grad_wk = left_dot(normed_one, grad_k_b)
    grad_wv = left_dot(normed_one, grad_v_b)
    grad_n1 = (
        right_dot(grad_q_b, wq_back) + right_dot(grad_k_b, wk_back) + right_dot(grad_v_b, wv_back)
    )
    grad_x_norm, grad_gain_one = norm_one_back(grad_n1)
    grad_tokens = (
        (grad_hidden + grad_x_norm).astype(jnp.bfloat16).reshape(shard_count, unit_max, width)
    )
    returned = lax.all_to_all(grad_tokens, "shard", split_axis=0, concat_axis=0, tiled=True)
    home_rows = (
        jnp.zeros(local_rows.shape, jnp.float32)
        .at[row_index]
        .add(jnp.where(sent_live[:, :, None], returned.astype(jnp.float32), 0.0))
    )
    grad_x = home_rows.astype(jnp.bfloat16)[None]
    attn_share = (
        lax.psum_scatter(
            grad_wq.astype(jnp.bfloat16), "shard", scatter_dimension=0, tiled=True
        ).astype(jnp.float32),
        lax.psum_scatter(
            grad_wk.astype(jnp.bfloat16), "shard", scatter_dimension=0, tiled=True
        ).astype(jnp.float32),
        lax.psum_scatter(
            grad_wv.astype(jnp.bfloat16), "shard", scatter_dimension=0, tiled=True
        ).astype(jnp.float32),
        lax.psum_scatter(
            grad_wo.astype(jnp.bfloat16), "shard", scatter_dimension=0, tiled=True
        ).astype(jnp.float32),
        lax.psum_scatter(
            grad_gain_one.astype(jnp.bfloat16), "shard", scatter_dimension=0, tiled=True
        ).astype(jnp.float32),
    )
    totals = (
        lax.psum(ffn_share[0].astype(jnp.bfloat16), "replica").astype(jnp.float32),
        lax.psum(ffn_share[1].astype(jnp.bfloat16), "replica").astype(jnp.float32),
        lax.psum(ffn_share[2].astype(jnp.bfloat16), "replica").astype(jnp.float32),
        lax.psum(ffn_share[3].astype(jnp.bfloat16), "replica").astype(jnp.float32),
        lax.psum(attn_share[0].astype(jnp.bfloat16), "replica").astype(jnp.float32),
        lax.psum(attn_share[1].astype(jnp.bfloat16), "replica").astype(jnp.float32),
        lax.psum(attn_share[2].astype(jnp.bfloat16), "replica").astype(jnp.float32),
        lax.psum(attn_share[3].astype(jnp.bfloat16), "replica").astype(jnp.float32),
        lax.psum(attn_share[4].astype(jnp.bfloat16), "replica").astype(jnp.float32),
    )
    return (
        layer_out,
        grad_x,
        totals[8],
        totals[3],
        totals[4],
        totals[5],
        totals[6],
        totals[7],
        totals[0],
        totals[1],
        totals[2],
    )


def solution(mesh):
    return jax.shard_map(
        shards,
        mesh=mesh,
        in_specs=(
            P("replica", "shard", None),
            P("replica", None),
            P("replica", None),
            P(),
            P("shard", None),
            P("shard", None),
            P("shard", None),
            P("shard", None),
            P(),
            P("shard", None),
            P("shard", None),
            P("shard", None),
            P("replica", "shard", None, None),
        ),
        out_specs=(
            P("replica", "shard", None, None),
            P("replica", "shard", None),
            P("shard"),
            P("shard"),
            P("shard", None),
            P("shard", None),
            P("shard", None),
            P("shard", None),
            P("shard", None),
            P("shard", None),
            P("shard", None),
        ),
        check_vma=False,
    )
```

profile of v0, /device:TPU:0, one launch (start us, length us, event | category | flops | bytes accessed | tf_op | source)
XLA Modules:
  0.0 894.3 jit_solution(441610172667195544)
XLA Ops:
  29.4 35.4 %all-to-all-done = bf16[16,64,768]{2,1,0:T(8,128)(2,1)S(1)} async-done(((bf16[16,64,768]{2,1,0:T(8,128)(2,1)}), bf16[16,64,768]{2,1,0:T(8,128)(2,1)S(1)}, u32[]{:S(2)}, u32[]{:S(2)}) %all-to-all-start) | async-done | bytes 1572896 | tf_op jit(solution)/shard_map/all_to_all | solution.py:150
  70.1 33.1 %all-gather.12.cloned.1.call-done = bf16[768,768]{1,0:T(8,128)(2,1)} async-done(((bf16[48,768]{1,0:T(8,128)(2,1)}), bf16[768,768]{1,0:T(8,128)(2,1)}) %all-gather.12.cloned.1.call-update) | async-done | bytes 1179664 | tf_op jit(solution)/shard_map/all_gather | solution.py:157
  106.5 10.7 %fusion.65 = f32[12,512,1024]{2,1,0:T(8,128)} fusion(bf16[512,12,64]{0,2,1:T(8,128)(2,1)S(1)} %bitcast.124, bf16[1024,12,64]{0,2,1:T(8,128)(2,1)S(1)} %bitcast.120), kind=kOutput, calls=%fused_computation.130 | convolution fusion | flops 805306368 | bytes 27525120 | tf_op jit(solution)/shard_map/qhd,khd->hqk/dot_general | solution.py:53
  117.2 16.7 %fusion.12 = (f32[12,512]{1,0:T(8,128)S(1)}, f32[12,512]{1,0:T(8,128)S(1)}, f32[12,512,1024]{2,1,0:T(8,128)}) fusion(pred[1024]{0:T(1024)(128)(4,1)S(1)} %broadcast_in_dim.135, f32[12,512,1024]{2,1,0:T(8,128)} %fusion.65, bf16[512,12,64]{0,2,1:T(8,128)(2,1)S(1)} %bitcast.130, bf16[1024,12,64]{0,2,1:T(8,128)(2,1)} %bitcast.121), kind=kOutput, calls=%fused_computation.26 | convolution fusion | flops 843042816 | bytes 52741120 | tf_op jit(solution)/shard_map/qhd,khd->hqk/dot_general | solution.py:53
  133.9 18.7 %fusion = (f32[12,512]{1,0:T(8,128)S(1)}, f32[12,512]{1,0:T(8,128)S(1)}) fusion(f32[12,512]{1,0:T(8,128)S(1)} %get-tuple-element.19, f32[12,512,1024]{2,1,0:T(8,128)} %get-tuple-element.47, pred[1024]{0:T(1024)(128)(4,1)S(1)} %broadcast_in_dim.135, f32[12,512]{1,0:T(8,128)S(1)} %get-tuple-element.20, f32[12,512,1024]{2,1,0:T(8,128)} %fusion.65), kind=kLoop, calls=%fused_computation.14 | loop fusion | flops 50319360 | bytes 50430976 | tf_op jit(solution)/shard_map/reduce_sum | solution.py:59
  155.8 11.7 %fusion.37 = bf16[12,64,512]{2,1,0:T(8,128)(2,1)S(1)} fusion(bf16[1024,12,64]{0,2,1:T(8,128)(2,1)S(1)} %bitcast.126, f32[12,512]{1,0:T(8,128)S(1)} %get-tuple-element.17, f32[12,512]{1,0:T(8,128)S(1)} %get-tuple-element.19, f32[12,512,1024]{2,1,0:T(8,128)} %get-tuple-element.47, pred[1024]{0:T(1024)(128)(4,1)S(1)} %broadcast_in_dim.135), kind=kOutput, calls=%fused_computation.87 | convolution fusion | flops 837156864 | bytes 27575296 | tf_op jit(solution)/shard_map/hqk,khd->qhd/dot_general | solution.py:61
  167.6 12.2 %fusion.36 = bf16[12,64,512]{2,1,0:T(8,128)(2,1)} fusion(bf16[1024,12,64]{0,2,1:T(8,128)(2,1)S(1)} %bitcast.127, f32[12,512]{1,0:T(8,128)S(1)} %get-tuple-element.18, f32[12,512]{1,0:T(8,128)S(1)} %get-tuple-element.20, f32[12,512,1024]{2,1,0:T(8,128)} %fusion.65, pred[1024]{0:T(1024)(128)(4,1)S(1)} %broadcast_in_dim.135), kind=kOutput, calls=%fused_computation.86 | convolution fusion | flops 837156864 | bytes 27575296 | tf_op jit(solution)/shard_map/hqk,khd->qhd/dot_general | solution.py:61
  187.8 40.9 %all-gather.18.cloned.1.call-done = bf16[768,2048]{1,0:T(8,128)(2,1)} async-done(((bf16[48,2048]{1,0:T(8,128)(2,1)}), bf16[768,2048]{1,0:T(8,128)(2,1)}) %all-gather.18.cloned.1.call-update) | async-done | bytes 3145744 | tf_op jit(solution)/shard_map/all_gather | solution.py:172
  236.1 38.5 %all-gather.16.cloned.1.call-done = bf16[768,2048]{1,0:T(8,128)(2,1)} async-done(((bf16[48,2048]{1,0:T(8,128)(2,1)}), bf16[768,2048]{1,0:T(8,128)(2,1)}) %all-gather.16.cloned.1.call-update) | async-done | bytes 3145744 | tf_op jit(solution)/shard_map/all_gather | solution.py:171
  274.7 9.0 %fusion.66 = f32[1024,2048]{1,0:T(8,128)} fusion(bf16[1024,768]{1,0:T(8,128)(2,1)} %copy-done.22, bf16[768,2048]{1,0:T(8,128)(2,1)} %all-gather.16.cloned.1.call-done), kind=kOutput, calls=%fused_computation.131 | convolution fusion | flops 3221225472 | bytes 13107200 | tf_op jit(solution)/shard_map/dot_general | solution.py:39
  283.7 37.1 %all-gather.20.cloned.1.call-done = bf16[2048,768]{1,0:T(8,128)(2,1)} async-done(((bf16[128,768]{1,0:T(8,128)(2,1)}), bf16[2048,768]{1,0:T(8,128)(2,1)}) %all-gather.20.cloned.1.call-update) | async-done | bytes 3145744 | tf_op jit(solution)/shard_map/all_gather | solution.py:173
  320.8 15.1 %multiply_convert_fusion.2 = (bf16[1024,2048]{1,0:T(8,128)(2,1)S(1)}, bf16[1024,2048]{1,0:T(8,128)(2,1)}, bf16[1024,2048]{1,0:T(8,128)(2,1)}) fusion(f32[1024,2048]{1,0:T(8,128)} %fusion.66, f32[1024,2048]{1,0:T(8,128)} %fusion.67, bf16[2048,768]{1,0:T(8,128)(2,1)} %all-gather.20.cloned.1.call-done, bf16[1,1,1024,768]{3,2,1,0:T(8,128)(2,1)S(1)} %copy-done.16, ...), kind=kOutput, calls=%fused_computation.35 | convolution fusion | flops 3278110720 | bytes 34079744 | tf_op jit(solution)/shard_map/dot_general | solution.py:33
  358.1 10.8 %fusion.69 = f32[12,512,1024]{2,1,0:T(8,128)} fusion(bf16[512,12,64]{0,2,1:T(8,128)(2,1)S(1)} %bitcast.132, bf16[1024,12,64]{0,2,1:T(8,128)(2,1)S(1)} %bitcast.128), kind=kOutput, calls=%fused_computation.134 | convolution fusion | flops 805306368 | bytes 27525120 | tf_op jit(solution)/shard_map/qhd,khd->hqk/dot_general | solution.py:87
  368.9 12.6 %fusion.4 = f32[12,64,1024]{2,1,0:T(8,128)} fusion(bf16[512,12,64]{0,2,1:T(8,128)(2,1)S(1)} %bitcast.133, f32[12,512]{1,0:T(8,128)S(1)} %get-tuple-element.53, f32[12,512,1024]{2,1,0:T(8,128)} %fusion.65, pred[1024]{0:T(1024)(128)(4,1)S(1)} %broadcast_in_dim.135), kind=kOutput, calls=%fused_computation.18 | convolution fusion | flops 830472192 | bytes 29123584 | tf_op jit(solution)/shard_map/hqk,qhd->khd/dot_general | solution.py:104
  381.5 35.6 %multiply_reduce_fusion.1 = (f32[12,512]{1,0:T(8,128)S(1)}, f32[12,512]{1,0:T(8,128)S(1)}, f32[12,512,1024]{2,1,0:T(8,128)}) fusion(f32[12,512]{1,0:T(8,128)S(1)} %get-tuple-element.54, f32[12,512,1024]{2,1,0:T(8,128)} %get-tuple-element.47, pred[1024]{0:T(1024)(128)(4,1)S(1)} %broadcast_in_dim.135, f32[12,512,1024]{2,1,0:T(8,128)} %fusion.69, ...), kind=kOutput, calls=%fused_computation.6 | convolution fusion | flops 868208640 | bytes 103121920 | tf_op jit(solution)/shard_map/qhd,khd->hqk/dot_general | solution.py:87
  417.1 12.3 %add_convert_fusion = bf16[12,64,1024]{2,1,0:T(8,128)(2,1)S(1)} fusion(f32[12,64,1024]{2,1,0:T(8,128)} %fusion.4, bf16[512,12,64]{0,2,1:T(8,128)(2,1)S(1)} %bitcast.138, f32[12,512]{1,0:T(8,128)S(1)} %get-tuple-element.54, f32[12,512,1024]{2,1,0:T(8,128)} %get-tuple-element.47, pred[1024]{0:T(1024)(128)(4,1)S(1)} %broadcast_in_dim.135), kind=kOutput, calls=%fused_computation.64 | convolution fusion | flops 832045056 | bytes 30696448 | tf_op jit(solution)/shard_map/hqk,qhd->khd/dot_general | solution.py:104
  433.1 42.5 %multiply_convert_fusion.1 = (bf16[12,512,1024]{2,1,0:T(8,128)(2,1)}, bf16[12,512,1024]{2,1,0:T(8,128)(2,1)}) fusion(f32[12,512,1024]{2,1,0:T(8,128)} %get-tuple-element.51, f32[12,512]{1,0:T(8,128)S(1)} %get-tuple-element.15, f32[12,512]{1,0:T(8,128)S(1)} %get-tuple-element.54, f32[12,512,1024]{2,1,0:T(8,128)} %get-tuple-element.47, ...), kind=kLoop, calls=%fused_computation.5 | loop fusion | flops 75497472 | bytes 125928448 | tf_op jit(solution)/shard_map/convert_element_type | solution.py:91
  484.3 8.7 multiply_convert_fusion.6
  552.7 60.4 %reduce-scatter.10.cloned.1.call-done = bf16[48,768]{1,0:T(8,128)(2,1)} async-done(((bf16[768,768]{1,0:T(8,128)(2,1)}), bf16[48,768]{1,0:T(8,128)(2,1)}) %reduce-scatter.10.cloned.1.call-update) | async-done | bytes 73744 | tf_op jit(solution)/shard_map/reduce_scatter | solution.py:250
  613.1 69.0 %reduce-scatter.20.cloned.1.call-done = bf16[128,768]{1,0:T(8,128)(2,1)} async-done(((bf16[2048,768]{1,0:T(8,128)(2,1)}), bf16[128,768]{1,0:T(8,128)(2,1)}) %reduce-scatter.20.cloned.1.call-update) | async-done | bytes 196624 | tf_op jit(solution)/shard_map/reduce_scatter | solution.py:206
  682.2 69.1 %reduce-scatter.16.cloned.1.call-done = bf16[48,2048]{1,0:T(8,128)(2,1)} async-done(((bf16[768,2048]{1,0:T(8,128)(2,1)}), bf16[48,2048]{1,0:T(8,128)(2,1)}) %reduce-scatter.16.cloned.1.call-update) | async-done | bytes 196624 | tf_op jit(solution)/shard_map/reduce_scatter | solution.py:200
  751.3 69.1 %reduce-scatter.18.cloned.1.call-done = bf16[48,2048]{1,0:T(8,128)(2,1)} async-done(((bf16[768,2048]{1,0:T(8,128)(2,1)}), bf16[48,2048]{1,0:T(8,128)(2,1)}) %reduce-scatter.18.cloned.1.call-update) | async-done | bytes 196624 | tf_op jit(solution)/shard_map/reduce_scatter | solution.py:203
  820.5 8.6 fusion.35
  829.1 29.5 %all-reduce.2 = (bf16[768]{0:T(1024)(128)(2,1)S(1)}, bf16[768]{0:T(1024)(128)(2,1)S(1)}) all-reduce(bf16[768]{0:T(1024)(128)(2,1)S(1)} %get-tuple-element.13, bf16[768]{0:T(1024)(128)(2,1)S(1)} %copy-done.36), channel_id=2, replica_groups=mesh['shard'=16,'replica'=2] {'shard'}, use_global_device_ids=true, to_apply=%region_16.17.clone | all-reduce | flops 1536 | bytes 6144
  (193 shorter events, 171.5 us)
Async XLA Ops:
  7.2 59.6 %all-gather.10.cloned.1.call-start = ((), (), s32[]{:S(2)}) async-start(), calls=%async_computation.10 | async-start | bytes 1253376 | tf_op jit(solution)/shard_map/all_gather | solution.py:156
  7.9 95.3 %all-gather.12.cloned.1.call-start = ((), (), s32[]{:S(2)}) async-start(), calls=%async_computation.11 | async-start | bytes 1253376 | tf_op jit(solution)/shard_map/all_gather | solution.py:157
  8.7 143.9 %all-gather.8.cloned.1.call-start = ((), (), s32[]{:S(2)}) async-start(), calls=%async_computation.9 | async-start | bytes 1253376 | tf_op jit(solution)/shard_map/all_gather | solution.py:158
  9.4 172.7 %all-gather.14.cloned.1.call-start = ((), (), s32[]{:S(2)}) async-start(), calls=%async_computation.12 | async-start | bytes 1253376 | tf_op jit(solution)/shard_map/all_gather | solution.py:159
  10.0 218.7 %all-gather.18.cloned.1.call-start = ((), (), s32[]{:S(2)}) async-start(), calls=%async_computation.14 | async-start | bytes 3342336 | tf_op jit(solution)/shard_map/all_gather | solution.py:172
  10.6 264.1 %all-gather.16.cloned.1.call-start = ((), (), s32[]{:S(2)}) async-start(), calls=%async_computation.13 | async-start | bytes 3342336 | tf_op jit(solution)/shard_map/all_gather | solution.py:171
  20.3 44.9 %copy-start.26 = (f32[768]{0:T(1024)S(1)}, f32[768]{0:T(1024)}, u32[]{:S(2)}) copy-start(f32[768]{0:T(1024)} %param.16) | copy-start | bytes 9220
  20.3 44.4 %all-to-all-start = ((bf16[16,64,768]{2,1,0:T(8,128)(2,1)}), bf16[16,64,768]{2,1,0:T(8,128)(2,1)S(1)}, u32[]{:S(2)}, u32[]{:S(2)}) async-start(bf16[16,64,768]{2,1,0:T(8,128)(2,1)} %broadcast_select_fusion), calls=%async_computation | async-start | bytes 3145728 | tf_op jit(solution)/shard_map/all_to_all | solution.py:150
  27.9 292.9 %all-gather.20.cloned.1.call-start = ((), (), s32[]{:S(2)}) async-start(), calls=%async_computation.15 | async-start | bytes 3342336 | tf_op jit(solution)/shard_map/all_gather | solution.py:173
  28.6 524.1 %reduce-scatter.14.cloned.1.call-start = ((), (), s32[]{:S(2)}) async-start(), calls=%async_computation.19 | async-start | bytes 1253376 | tf_op jit(solution)/shard_map/reduce_scatter | solution.py:256
  64.8 120.6 %copy-start.2 = (bf16[16,64,768]{2,1,0:T(8,128)(2,1)}, bf16[16,64,768]{2,1,0:T(8,128)(2,1)S(1)}, u32[]{:S(2)}) copy-start(bf16[16,64,768]{2,1,0:T(8,128)(2,1)S(1)} %all-to-all-done) | copy-start | bytes 4718596
  70.1 47.1 %copy-start.14 = (bf16[512,768]{0,1:T(8,128)(2,1)}, bf16[512,768]{0,1:T(8,128)(2,1)S(1)}, u32[]{:S(2)}) copy-start(bf16[512,768]{0,1:T(8,128)(2,1)S(1)} %get-tuple-element.40) | copy-start | bytes 2359300
  187.8 40.9 %copy-start.22 = (bf16[1024,768]{1,0:T(8,128)(2,1)}, bf16[1024,768]{1,0:T(8,128)(2,1)S(1)}, u32[]{:S(2)}) copy-start(bf16[1024,768]{1,0:T(8,128)(2,1)S(1)} %multiply_convert_fusion.5) | copy-start | bytes 4718596
  236.1 84.7 %copy-start.16 = (bf16[1,1,1024,768]{3,2,1,0:T(8,128)(2,1)S(1)}, bf16[1,1,1024,768]{3,2,1,0:T(8,128)(2,1)}, u32[]{:S(2)}) copy-start(bf16[1,1,1024,768]{3,2,1,0:T(8,128)(2,1)} %param.25) | copy-start | bytes 4718596
  353.3 199.4 %reduce-scatter.12.cloned.1.call-start = ((), (), s32[]{:S(2)}) async-start(), calls=%async_computation.18 | async-start | bytes 1253376 | tf_op jit(solution)/shard_map/reduce_scatter | solution.py:253
  433.1 119.6 %reduce-scatter.8.cloned.1.call-start = ((), (), s32[]{:S(2)}) async-start(), calls=%async_computation.16 | async-start | bytes 1253376 | tf_op jit(solution)/shard_map/reduce_scatter | solution.py:247
  433.1 42.6 %copy-start.5 = (bf16[1024,768]{0,1:T(8,128)(2,1)S(1)}, bf16[1024,768]{0,1:T(8,128)(2,1)}, u32[]{:S(2)}) copy-start(bf16[1024,768]{0,1:T(8,128)(2,1)} %copy-done.4) | copy-start | bytes 4718596
  495.4 117.7 %reduce-scatter.10.cloned.1.call-start = ((), (), s32[]{:S(2)}) async-start(), calls=%async_computation.17 | async-start | bytes 1253376 | tf_op jit(solution)/shard_map/reduce_scatter | solution.py:250
  512.4 169.8 %reduce-scatter.20.cloned.1.call-start = ((), (), s32[]{:S(2)}) async-start(), calls=%async_computation.22 | async-start | bytes 3342336 | tf_op jit(solution)/shard_map/reduce_scatter | solution.py:206
  520.4 230.9 %reduce-scatter.16.cloned.1.call-start = ((), (), s32[]{:S(2)}) async-start(), calls=%async_computation.20 | async-start | bytes 3342336 | tf_op jit(solution)/shard_map/reduce_scatter | solution.py:200
  528.4 292.1 %reduce-scatter.18.cloned.1.call-start = ((), (), s32[]{:S(2)}) async-start(), calls=%async_computation.21 | async-start | bytes 3342336 | tf_op jit(solution)/shard_map/reduce_scatter | solution.py:203
  547.3 317.4 %all-to-all-start.1 = ((bf16[16,64,768]{2,1,0:T(8,128)(2,1)}), bf16[16,64,768]{2,1,0:T(8,128)(2,1)S(1)}, u32[]{:S(2)}, u32[]{:S(2)}) async-start(bf16[16,64,768]{2,1,0:T(8,128)(2,1)} %bitcast.26), calls=%async_computation.1 | async-start | bytes 3145728 | tf_op jit(solution)/shard_map/all_to_all | solution.py:239
  551.2 325.1 %all-reduce.7.cloned.1.call-start = ((), (), s32[]{:S(2)}) async-start(), calls=%async_computation.23 | async-start | bytes 1769472 | tf_op jit(solution)/shard_map/psum | solution.py:268
  820.5 44.2 %copy-start.33 = (pred[16,64]{1,0:T(8,128)(4,1)S(1)}, pred[16,64]{1,0:T(8,128)(4,1)}, u32[]{:S(2)}) copy-start(pred[16,64]{1,0:T(8,128)(4,1)} %copy-done.32) | copy-start | bytes 3076
  (37 other events, 217.4 us)
Sparse Core Ops, SparseCore 0:
  10.3 51.5 all-gather.9
  64.1 39.0 all-gather.11
  105.6 37.1 all-gather.7
  144.9 37.1 all-gather.13
  184.2 44.3 all-gather.17
  230.8 43.8 all-gather.15
  276.9 43.8 all-gather.19
  353.5 56.5 reduce-scatter.13
  433.2 56.6 reduce-scatter.11
  495.5 56.5 reduce-scatter.7
  555.8 57.3 reduce-scatter.9
  616.8 65.3 reduce-scatter.19
  686.0 65.2 reduce-scatter.15
  755.0 65.4 reduce-scatter.17
  823.0 35.4 all-reduce.6
where the time goes:
time: 900 us; the launch traced here: 894 us
  waiting for transfers between devices  460 us (51%)
  matrix products  262 us (29%)
  other arithmetic  97.7 us (11%)
  blocking collectives  34.4 us (4%)
  between operations  15.4 us (2%)
  starting transfers between devices  12.7 us (1%)
  local copies, waits for them, and re-layouts  12.1 us (1%)
    reduce_scatter x1, waiting for transfers between devices, shards(): lax.psum_scatter(grad_wg.astype(jnp.bfloat16), 'shard', scatter_dimension...  69.1 us
    reduce_scatter x1, waiting for transfers between devices, shards(): lax.psum_scatter(grad_wu.astype(jnp.bfloat16), 'shard', scatter_dimension...  69.1 us
    reduce_scatter x1, waiting for transfers between devices, shards(): lax.psum_scatter(grad_down.astype(jnp.bfloat16), 'shard', scatter_dimensi...  69 us
    reduce_scatter x1, waiting for transfers between devices, shards(): lax.psum_scatter(grad_wk.astype(jnp.bfloat16), 'shard', scatter_dimension...  60.4 us
    dot_general x2, matrix products, attend_backward(): jnp.einsum('qhd,khd->hqk', grad_heads, value_heads, preferred_element_typ...  46.4 us
    convert_element_type x1, other arithmetic, attend_backward(): grad_scores = (prob_vals * (grad_probs - row_dot)).astype(jnp.bfloat16)  42.5 us
    all_gather x1, waiting for transfers between devices, shards(): lax.all_gather(w_up, 'shard', axis=0, tiled=True)  40.9 us
    all_gather x1, waiting for transfers between devices, shards(): lax.all_gather(w_gate, 'shard', axis=0, tiled=True)  38.5 us
  transfers between devices with their start and end apart: 17, of which 10 were waited for; matrix products, arithmetic and copies ran while one was open for 36% of the time, Pallas kernels for 0%

commit v1 on v0

--- a/solution.py
+++ b/solution.py
@@ -7,6 +7,34 @@
 HD = 64
 norm_eps = 1e-06
 neg_big = -1e30
+
+
+def report_leaf_up(u, along_dim, page):
+    e_next = u.shape
+    before = u.reshape(
+        *e_next[:along_dim], page, e_next[along_dim] // page, *e_next[along_dim + 1 :]
+    )
+    return jnp.moveaxis(before, along_dim, 0)
+
+
+def map_the_matrix(t0, axis_k):
+    t0 = jnp.moveaxis(t0, 0, axis_k)
+    g_now = t0.shape
+    return t0.reshape(*g_now[:axis_k], g_now[axis_k] * g_now[axis_k + 1], *g_now[axis_k + 2 :])
+
+
+def slot_solve(raw, axis_key, field, body):
+    b_next = lax.axis_size(axis_key)
+    right_arr = lax.axis_index(axis_key)
+    f_next, a_next = (b_next, right_arr)
+    met_up = report_leaf_up(raw, field, f_next)
+    pieces_in = [met_up[a_next]]
+    for j0 in range(1, f_next):
+        earlier = met_up[a_next ^ j0]
+        pieces_in.append(lax.ppermute(earlier, axis_key, [(i, i ^ j0) for i in range(f_next)]))
+    carry_in = jnp.stack(pieces_in, 0)
+    met_up = carry_in[a_next ^ jnp.arange(f_next)]
+    return map_the_matrix(met_up, body)
 
 
 def rms_scale(tok_rows, gain_vec):
@@ -147,7 +175,7 @@
     outgoing = jnp.where(
         sent_live[:, :, None], local_rows[row_index], jnp.zeros((), local_rows.dtype)
     )
-    arrived = lax.all_to_all(outgoing, "shard", split_axis=0, concat_axis=0, tiled=True)
+    arrived = slot_solve(outgoing, "shard", 0, 0)
     own_count = jnp.sum(jnp.where(dest_idx == my_index, counts, 0))
     live_rows = jnp.broadcast_to(inner_idx[None, :] < own_count, (shard_count, unit_max)).reshape(
         span

time: 900 us -> 901 us (level)
  waiting for transfers between devices: 460 us -> 443 us
  starting transfers between devices: 12.7 us -> 23.2 us
    ppermute x0 -> x15, waiting for transfers between devices: none -> 58.2 us  [slot_solve(): lax.ppermute(earlier, axis_key, [(i, i ^ j0) for i in range(f_next)])]
    all_to_all x1 -> x0, waiting for transfers between devices: 35.4 us -> none  [shards(): lax.all_to_all(outgoing, 'shard', split_axis=0, concat_axis=0, tiled=True)]
    all_gather x1, waiting for transfers between devices: 33.1 us -> 0.02 us  [shards(): lax.all_gather(w_key, 'shard', axis=0, tiled=True)]
    ppermute x0 -> x15, starting transfers between devices: none -> 18 us  [slot_solve(): lax.ppermute(earlier, axis_key, [(i, i ^ j0) for i in range(f_next)])]
  transfers between devices with their start and end apart: 17 -> 31, of which waited for: 10 -> 17; matrix products, arithmetic and copies ran while one was open for 36% -> 36% of each run, Pallas kernels for 0% -> 0%
where the time goes in v1:
time: 901 us; the launch traced here: 895 us
  waiting for transfers between devices  443 us (49%)
  matrix products  263 us (29%)
  other arithmetic  96.5 us (11%)
  blocking collectives  34.4 us (4%)
  starting transfers between devices  23.2 us (3%)
  local copies, waits for them, and re-layouts  19.1 us (2%)
  between operations  15.6 us (2%)
    reduce_scatter x1, waiting for transfers between devices, shards(): lax.psum_scatter(grad_wg.astype(jnp.bfloat16), 'shard', scatter_dimension...  69.1 us
    reduce_scatter x1, waiting for transfers between devices, shards(): lax.psum_scatter(grad_down.astype(jnp.bfloat16), 'shard', scatter_dimensi...  69 us
    reduce_scatter x1, waiting for transfers between devices, shards(): lax.psum_scatter(grad_wu.astype(jnp.bfloat16), 'shard', scatter_dimension...  69 us
    reduce_scatter x1, waiting for transfers between devices, shards(): lax.psum_scatter(grad_wk.astype(jnp.bfloat16), 'shard', scatter_dimension...  60.5 us
    ppermute x15, waiting for transfers between devices, slot_solve(): lax.ppermute(earlier, axis_key, [(i, i ^ j0) for i in range(f_next)])  58.2 us
    dot_general x2, matrix products, attend_backward(): jnp.einsum('qhd,khd->hqk', grad_heads, value_heads, preferred_element_typ...  46.4 us
    convert_element_type x1, other arithmetic, attend_backward(): grad_scores = (prob_vals * (grad_probs - row_dot)).astype(jnp.bfloat16)  42.7 us
    all_gather x1, waiting for transfers between devices, shards(): lax.all_gather(w_gate, 'shard', axis=0, tiled=True)  38.5 us
  transfers between devices with their start and end apart: 31, of which 17 were waited for; matrix products, arithmetic and copies ran while one was open for 36% of the time, Pallas kernels for 0%

profile of v1, /device:TPU:0, one launch (start us, length us, event | category | flops | bytes accessed | tf_op | source)
XLA Modules:
  0.0 894.9 jit_solution(13076250737856059809)
XLA Ops:
  72.6 9.1 %collective-permute-done.8 = bf16[1,64,768]{2,1,0:T(8,128)(2,1)S(1)} collective-permute-done((bf16[1,64,768]{2,1,0:T(8,128)(2,1)S(1)}, bf16[1,64,768]{2,1,0:T(8,128)(2,1)S(1)}, u32[]{:S(2)}, u32[]{:S(2)}) %collective-permute-start.8) | collective-permute-done | bytes 98336 | tf_op jit(solution)/shard_map/ppermute | solution.py:34
  88.5 10.2 %collective-permute-done.10 = bf16[1,64,768]{2,1,0:T(8,128)(2,1)S(1)} collective-permute-done((bf16[1,64,768]{2,1,0:T(8,128)(2,1)S(1)}, bf16[1,64,768]{2,1,0:T(8,128)(2,1)S(1)}, u32[]{:S(2)}, u32[]{:S(2)}) %collective-permute-start.10) | collective-permute-done | bytes 98336 | tf_op jit(solution)/shard_map/ppermute | solution.py:34
  112.7 10.7 %fusion.66 = f32[12,512,1024]{2,1,0:T(8,128)} fusion(bf16[512,12,64]{0,2,1:T(8,128)(2,1)S(1)} %bitcast.168, bf16[1024,12,64]{0,2,1:T(8,128)(2,1)S(1)} %bitcast.164), kind=kOutput, calls=%fused_computation.165 | convolution fusion | flops 805306368 | bytes 27525120 | tf_op jit(solution)/shard_map/qhd,khd->hqk/dot_general | solution.py:81
  123.4 16.7 %fusion.12 = (f32[12,512]{1,0:T(8,128)S(1)}, f32[12,512]{1,0:T(8,128)S(1)}, f32[12,512,1024]{2,1,0:T(8,128)}) fusion(pred[1024]{0:T(1024)(128)(4,1)S(1)} %broadcast_in_dim.138, f32[12,512,1024]{2,1,0:T(8,128)} %fusion.66, bf16[512,12,64]{0,2,1:T(8,128)(2,1)S(1)} %bitcast.174, bf16[1024,12,64]{0,2,1:T(8,128)(2,1)} %bitcast.165), kind=kOutput, calls=%fused_computation.27 | convolution fusion | flops 843042816 | bytes 52741120 | tf_op jit(solution)/shard_map/qhd,khd->hqk/dot_general | solution.py:81
  140.1 18.7 %fusion = (f32[12,512]{1,0:T(8,128)S(1)}, f32[12,512]{1,0:T(8,128)S(1)}) fusion(f32[12,512]{1,0:T(8,128)S(1)} %get-tuple-element.19, f32[12,512,1024]{2,1,0:T(8,128)} %get-tuple-element.62, pred[1024]{0:T(1024)(128)(4,1)S(1)} %broadcast_in_dim.138, f32[12,512]{1,0:T(8,128)S(1)} %get-tuple-element.20, f32[12,512,1024]{2,1,0:T(8,128)} %fusion.66), kind=kLoop, calls=%fused_computation.15 | loop fusion | flops 50319360 | bytes 50430976 | tf_op jit(solution)/shard_map/reduce_sum | solution.py:87
  162.0 11.7 %fusion.37 = bf16[12,64,512]{2,1,0:T(8,128)(2,1)S(1)} fusion(bf16[1024,12,64]{0,2,1:T(8,128)(2,1)S(1)} %bitcast.170, f32[12,512]{1,0:T(8,128)S(1)} %get-tuple-element.17, f32[12,512]{1,0:T(8,128)S(1)} %get-tuple-element.19, f32[12,512,1024]{2,1,0:T(8,128)} %get-tuple-element.62, pred[1024]{0:T(1024)(128)(4,1)S(1)} %broadcast_in_dim.138), kind=kOutput, calls=%fused_computation.88 | convolution fusion | flops 837156864 | bytes 27575296 | tf_op jit(solution)/shard_map/hqk,khd->qhd/dot_general | solution.py:89
  173.7 12.3 %fusion.36 = bf16[12,64,512]{2,1,0:T(8,128)(2,1)} fusion(bf16[1024,12,64]{0,2,1:T(8,128)(2,1)S(1)} %bitcast.171, f32[12,512]{1,0:T(8,128)S(1)} %get-tuple-element.18, f32[12,512]{1,0:T(8,128)S(1)} %get-tuple-element.20, f32[12,512,1024]{2,1,0:T(8,128)} %fusion.66, pred[1024]{0:T(1024)(128)(4,1)S(1)} %broadcast_in_dim.138), kind=kOutput, calls=%fused_computation.87 | convolution fusion | flops 837156864 | bytes 27575296 | tf_op jit(solution)/shard_map/hqk,khd->qhd/dot_general | solution.py:89
  191.3 38.0 %all-gather.18.cloned.1.call-done = bf16[768,2048]{1,0:T(8,128)(2,1)} async-done(((bf16[48,2048]{1,0:T(8,128)(2,1)}), bf16[768,2048]{1,0:T(8,128)(2,1)}) %all-gather.18.cloned.1.call-update) | async-done | bytes 3145744 | tf_op jit(solution)/shard_map/all_gather | solution.py:200
  236.8 38.5 %all-gather.16.cloned.1.call-done = bf16[768,2048]{1,0:T(8,128)(2,1)} async-done(((bf16[48,2048]{1,0:T(8,128)(2,1)}), bf16[768,2048]{1,0:T(8,128)(2,1)}) %all-gather.16.cloned.1.call-update) | async-done | bytes 3145744 | tf_op jit(solution)/shard_map/all_gather | solution.py:199
  275.3 9.0 %fusion.67 = f32[1024,2048]{1,0:T(8,128)} fusion(bf16[1024,768]{1,0:T(8,128)(2,1)} %copy-done.24, bf16[768,2048]{1,0:T(8,128)(2,1)} %all-gather.16.cloned.1.call-done), kind=kOutput, calls=%fused_computation.166 | convolution fusion | flops 3221225472 | bytes 13107200 | tf_op jit(solution)/shard_map/dot_general | solution.py:67
  284.3 37.1 %all-gather.20.cloned.1.call-done = bf16[2048,768]{1,0:T(8,128)(2,1)} async-done(((bf16[128,768]{1,0:T(8,128)(2,1)}), bf16[2048,768]{1,0:T(8,128)(2,1)}) %all-gather.20.cloned.1.call-update) | async-done | bytes 3145744 | tf_op jit(solution)/shard_map/all_gather | solution.py:201
  321.4 15.1 %multiply_convert_fusion.2 = (bf16[1024,2048]{1,0:T(8,128)(2,1)S(1)}, bf16[1024,2048]{1,0:T(8,128)(2,1)}, bf16[1024,2048]{1,0:T(8,128)(2,1)}) fusion(f32[1024,2048]{1,0:T(8,128)} %fusion.67, f32[1024,2048]{1,0:T(8,128)} %fusion.68, bf16[2048,768]{1,0:T(8,128)(2,1)} %all-gather.20.cloned.1.call-done, bf16[1,1,1024,768]{3,2,1,0:T(8,128)(2,1)S(1)} %copy-done.18, ...), kind=kOutput, calls=%fused_computation.36 | convolution fusion | flops 3278110720 | bytes 34079744 | tf_op jit(solution)/shard_map/dot_general | solution.py:61
  358.7 10.9 %fusion.70 = f32[12,512,1024]{2,1,0:T(8,128)} fusion(bf16[512,12,64]{0,2,1:T(8,128)(2,1)S(1)} %bitcast.176, bf16[1024,12,64]{0,2,1:T(8,128)(2,1)S(1)} %bitcast.172), kind=kOutput, calls=%fused_computation.169 | convolution fusion | flops 805306368 | bytes 27525120 | tf_op jit(solution)/shard_map/qhd,khd->hqk/dot_general | solution.py:115
  369.5 12.6 %fusion.4 = f32[12,64,1024]{2,1,0:T(8,128)} fusion(bf16[512,12,64]{0,2,1:T(8,128)(2,1)S(1)} %bitcast.177, f32[12,512]{1,0:T(8,128)S(1)} %get-tuple-element.68, f32[12,512,1024]{2,1,0:T(8,128)} %fusion.66, pred[1024]{0:T(1024)(128)(4,1)S(1)} %broadcast_in_dim.138), kind=kOutput, calls=%fused_computation.19 | convolution fusion | flops 830472192 | bytes 29123584 | tf_op jit(solution)/shard_map/hqk,qhd->khd/dot_general | solution.py:132
  382.1 35.6 %multiply_reduce_fusion.1 = (f32[12,512]{1,0:T(8,128)S(1)}, f32[12,512]{1,0:T(8,128)S(1)}, f32[12,512,1024]{2,1,0:T(8,128)}) fusion(f32[12,512]{1,0:T(8,128)S(1)} %get-tuple-element.69, f32[12,512,1024]{2,1,0:T(8,128)} %get-tuple-element.62, pred[1024]{0:T(1024)(128)(4,1)S(1)} %broadcast_in_dim.138, f32[12,512,1024]{2,1,0:T(8,128)} %fusion.70, ...), kind=kOutput, calls=%fused_computation.7 | convolution fusion | flops 868208640 | bytes 103121920 | tf_op jit(solution)/shard_map/qhd,khd->hqk/dot_general | solution.py:115
  417.7 12.3 %add_convert_fusion = bf16[12,64,1024]{2,1,0:T(8,128)(2,1)S(1)} fusion(f32[12,64,1024]{2,1,0:T(8,128)} %fusion.4, bf16[512,12,64]{0,2,1:T(8,128)(2,1)S(1)} %bitcast.182, f32[12,512]{1,0:T(8,128)S(1)} %get-tuple-element.69, f32[12,512,1024]{2,1,0:T(8,128)} %get-tuple-element.62, pred[1024]{0:T(1024)(128)(4,1)S(1)} %broadcast_in_dim.138), kind=kOutput, calls=%fused_computation.65 | convolution fusion | flops 832045056 | bytes 30696448 | tf_op jit(solution)/shard_map/hqk,qhd->khd/dot_general | solution.py:132
  433.7 42.7 %multiply_convert_fusion.1 = (bf16[12,512,1024]{2,1,0:T(8,128)(2,1)}, bf16[12,512,1024]{2,1,0:T(8,128)(2,1)}) fusion(f32[12,512,1024]{2,1,0:T(8,128)} %get-tuple-element.66, f32[12,512]{1,0:T(8,128)S(1)} %get-tuple-element.15, f32[12,512]{1,0:T(8,128)S(1)} %get-tuple-element.69, f32[12,512,1024]{2,1,0:T(8,128)} %get-tuple-element.62, ...), kind=kLoop, calls=%fused_computation.6 | loop fusion | flops 75497472 | bytes 125928448 | tf_op jit(solution)/shard_map/convert_element_type | solution.py:119
  484.9 8.7 multiply_convert_fusion.6
  553.5 60.5 %reduce-scatter.10.cloned.1.call-done = bf16[48,768]{1,0:T(8,128)(2,1)} async-done(((bf16[768,768]{1,0:T(8,128)(2,1)}), bf16[48,768]{1,0:T(8,128)(2,1)}) %reduce-scatter.10.cloned.1.call-update) | async-done | bytes 73744 | tf_op jit(solution)/shard_map/reduce_scatter | solution.py:278
  613.9 69.0 %reduce-scatter.20.cloned.1.call-done = bf16[128,768]{1,0:T(8,128)(2,1)} async-done(((bf16[2048,768]{1,0:T(8,128)(2,1)}), bf16[128,768]{1,0:T(8,128)(2,1)}) %reduce-scatter.20.cloned.1.call-update) | async-done | bytes 196624 | tf_op jit(solution)/shard_map/reduce_scatter | solution.py:234
  682.9 69.1 %reduce-scatter.16.cloned.1.call-done = bf16[48,2048]{1,0:T(8,128)(2,1)} async-done(((bf16[768,2048]{1,0:T(8,128)(2,1)}), bf16[48,2048]{1,0:T(8,128)(2,1)}) %reduce-scatter.16.cloned.1.call-update) | async-done | bytes 196624 | tf_op jit(solution)/shard_map/reduce_scatter | solution.py:228
  752.0 69.0 %reduce-scatter.18.cloned.1.call-done = bf16[48,2048]{1,0:T(8,128)(2,1)} async-done(((bf16[768,2048]{1,0:T(8,128)(2,1)}), bf16[48,2048]{1,0:T(8,128)(2,1)}) %reduce-scatter.18.cloned.1.call-update) | async-done | bytes 196624 | tf_op jit(solution)/shard_map/reduce_scatter | solution.py:231
  821.0 8.6 fusion.35
  829.6 29.5 %all-reduce.2 = (bf16[768]{0:T(1024)(128)(2,1)S(1)}, bf16[768]{0:T(1024)(128)(2,1)S(1)}) all-reduce(bf16[768]{0:T(1024)(128)(2,1)S(1)} %get-tuple-element.13, bf16[768]{0:T(1024)(128)(2,1)S(1)} %copy-done.38), channel_id=2, replica_groups=mesh['shard'=16,'replica'=2] {'shard'}, use_global_device_ids=true, to_apply=%region_16.17.clone | all-reduce | flops 1536 | bytes 6144
  (245 shorter events, 223.9 us)
Async XLA Ops:
  7.2 98.4 %all-gather.10.cloned.1.call-start = ((), (), s32[]{:S(2)}) async-start(), calls=%async_computation.9 | async-start | bytes 1253376 | tf_op jit(solution)/shard_map/all_gather | solution.py:184
  7.9 101.0 %all-gather.12.cloned.1.call-start = ((), (), s32[]{:S(2)}) async-start(), calls=%async_computation.10 | async-start | bytes 1253376 | tf_op jit(solution)/shard_map/all_gather | solution.py:185
  8.7 150.1 %all-gather.8.cloned.1.call-start = ((), (), s32[]{:S(2)}) async-start(), calls=%async_computation.8 | async-start | bytes 1253376 | tf_op jit(solution)/shard_map/all_gather | solution.py:186
  9.4 176.6 %all-gather.14.cloned.1.call-start = ((), (), s32[]{:S(2)}) async-start(), calls=%async_computation.11 | async-start | bytes 1253376 | tf_op jit(solution)/shard_map/all_gather | solution.py:187
  10.0 219.3 %all-gather.18.cloned.1.call-start = ((), (), s32[]{:S(2)}) async-start(), calls=%async_computation.13 | async-start | bytes 3342336 | tf_op jit(solution)/shard_map/all_gather | solution.py:200
  10.6 264.7 %all-gather.16.cloned.1.call-start = ((), (), s32[]{:S(2)}) async-start(), calls=%async_computation.12 | async-start | bytes 3342336 | tf_op jit(solution)/shard_map/all_gather | solution.py:199
  11.2 310.2 %all-gather.20.cloned.1.call-start = ((), (), s32[]{:S(2)}) async-start(), calls=%async_computation.14 | async-start | bytes 3342336 | tf_op jit(solution)/shard_map/all_gather | solution.py:201
  20.6 78.1 %collective-permute-start.14 = (bf16[1,64,768]{2,1,0:T(8,128)(2,1)S(1)}, bf16[1,64,768]{2,1,0:T(8,128)(2,1)S(1)}, u32[]{:S(2)}, u32[]{:S(2)}) collective-permute-start(bf16[1,64,768]{2,1,0:T(8,128)(2,1)S(1)} %get-tuple-element.41), channel_id=1, source_target_pairs={{0,30},{2,28},{4,26},{6,24},{8,22},{10,20},{12,18},{14,16},{16,14}... | collective-permute-start | bytes 294920 | tf_op jit(solution)/shard_map/ppermute | solution.py:34
  26.1 72.6 %collective-permute-start.13 = (bf16[1,64,768]{2,1,0:T(8,128)(2,1)S(1)}, bf16[1,64,768]{2,1,0:T(8,128)(2,1)S(1)}, u32[]{:S(2)}, u32[]{:S(2)}) collective-permute-start(bf16[1,64,768]{2,1,0:T(8,128)(2,1)S(1)} %get-tuple-element.42), channel_id=1, source_target_pairs={{0,28},{2,30},{4,24},{6,26},{8,20},{10,22},{12,16},{14,18},{16,12}... | collective-permute-start | bytes 294920 | tf_op jit(solution)/shard_map/ppermute | solution.py:34
  26.7 71.9 %collective-permute-start.12 = (bf16[1,64,768]{2,1,0:T(8,128)(2,1)S(1)}, bf16[1,64,768]{2,1,0:T(8,128)(2,1)S(1)}, u32[]{:S(2)}, u32[]{:S(2)}) collective-permute-start(bf16[1,64,768]{2,1,0:T(8,128)(2,1)S(1)} %get-tuple-element.43), channel_id=1, source_target_pairs={{0,26},{2,24},{4,30},{6,28},{8,18},{10,16},{12,22},{14,20},{16,10}... | collective-permute-start | bytes 294920 | tf_op jit(solution)/shard_map/ppermute | solution.py:34
  29.9 68.7 %collective-permute-start.11 = (bf16[1,64,768]{2,1,0:T(8,128)(2,1)S(1)}, bf16[1,64,768]{2,1,0:T(8,128)(2,1)S(1)}, u32[]{:S(2)}, u32[]{:S(2)}) collective-permute-start(bf16[1,64,768]{2,1,0:T(8,128)(2,1)S(1)} %get-tuple-element.44), channel_id=1, source_target_pairs={{0,24},{2,26},{4,28},{6,30},{8,16},{10,18},{12,20},{14,22},{16,8},... | collective-permute-start | bytes 294920 | tf_op jit(solution)/shard_map/ppermute | solution.py:34
  30.4 523.0 %reduce-scatter.14.cloned.1.call-start = ((), (), s32[]{:S(2)}) async-start(), calls=%async_computation.18 | async-start | bytes 1253376 | tf_op jit(solution)/shard_map/reduce_scatter | solution.py:284
  64.0 8.6 collective-permute-start.7
  72.6 9.2 %collective-permute-start.8 = (bf16[1,64,768]{2,1,0:T(8,128)(2,1)S(1)}, bf16[1,64,768]{2,1,0:T(8,128)(2,1)S(1)}, u32[]{:S(2)}, u32[]{:S(2)}) collective-permute-start(bf16[1,64,768]{2,1,0:T(8,128)(2,1)S(1)} %get-tuple-element.47), channel_id=1, source_target_pairs={{0,18},{2,16},{4,22},{6,20},{8,26},{10,24},{12,30},{14,28},{16,2},... | collective-permute-start | bytes 294920 | tf_op jit(solution)/shard_map/ppermute | solution.py:34
  81.7 6.7 collective-permute-start.9
  88.5 10.2 %collective-permute-start.10 = (bf16[1,64,768]{2,1,0:T(8,128)(2,1)S(1)}, bf16[1,64,768]{2,1,0:T(8,128)(2,1)S(1)}, u32[]{:S(2)}, u32[]{:S(2)}) collective-permute-start(bf16[1,64,768]{2,1,0:T(8,128)(2,1)S(1)} %get-tuple-element.45), channel_id=1, source_target_pairs={{0,22},{2,20},{4,18},{6,16},{8,30},{10,28},{12,26},{14,24},{16,6},... | collective-permute-start | bytes 294920 | tf_op jit(solution)/shard_map/ppermute | solution.py:34
  353.9 199.6 %reduce-scatter.12.cloned.1.call-start = ((), (), s32[]{:S(2)}) async-start(), calls=%async_computation.17 | async-start | bytes 1253376 | tf_op jit(solution)/shard_map/reduce_scatter | solution.py:281
  433.6 119.8 %reduce-scatter.8.cloned.1.call-start = ((), (), s32[]{:S(2)}) async-start(), calls=%async_computation.15 | async-start | bytes 1253376 | tf_op jit(solution)/shard_map/reduce_scatter | solution.py:275
  496.1 117.8 %reduce-scatter.10.cloned.1.call-start = ((), (), s32[]{:S(2)}) async-start(), calls=%async_computation.16 | async-start | bytes 1253376 | tf_op jit(solution)/shard_map/reduce_scatter | solution.py:278
  513.1 169.8 %reduce-scatter.20.cloned.1.call-start = ((), (), s32[]{:S(2)}) async-start(), calls=%async_computation.21 | async-start | bytes 3342336 | tf_op jit(solution)/shard_map/reduce_scatter | solution.py:234
  521.1 230.9 %reduce-scatter.16.cloned.1.call-start = ((), (), s32[]{:S(2)}) async-start(), calls=%async_computation.19 | async-start | bytes 3342336 | tf_op jit(solution)/shard_map/reduce_scatter | solution.py:228
  529.1 291.9 %reduce-scatter.18.cloned.1.call-start = ((), (), s32[]{:S(2)}) async-start(), calls=%async_computation.20 | async-start | bytes 3342336 | tf_op jit(solution)/shard_map/reduce_scatter | solution.py:231
  548.1 317.2 %all-to-all-start = ((bf16[16,64,768]{2,1,0:T(8,128)(2,1)}), bf16[16,64,768]{2,1,0:T(8,128)(2,1)S(1)}, u32[]{:S(2)}, u32[]{:S(2)}) async-start(bf16[16,64,768]{2,1,0:T(8,128)(2,1)} %bitcast.45), calls=%async_computation | async-start | bytes 3145728 | tf_op jit(solution)/shard_map/all_to_all | solution.py:267
  551.9 324.9 %all-reduce.7.cloned.1.call-start = ((), (), s32[]{:S(2)}) async-start(), calls=%async_computation.22 | async-start | bytes 1769472 | tf_op jit(solution)/shard_map/psum | solution.py:296
  (53 other events, 564.5 us)
Sparse Core Ops, SparseCore 0:
  10.3 50.2 all-gather.9
  62.9 40.9 all-gather.11
  106.1 37.2 all-gather.7
  145.5 37.1 all-gather.13
  184.9 44.3 all-gather.17
  231.4 43.8 all-gather.15
  277.5 43.8 all-gather.19
  354.0 56.4 reduce-scatter.13
  433.7 56.5 reduce-scatter.11
  496.2 56.5 reduce-scatter.7
  556.5 57.4 reduce-scatter.9
  617.6 65.2 reduce-scatter.19
  686.7 65.2 reduce-scatter.15
  755.7 65.2 reduce-scatter.17
  823.5 35.5 all-reduce.6
